TPU v7x, 32 devices: a whole 2x2x4 slice. The times are simulated.
32 devices in a mesh: seq: 8 (over y, x, core), tp: 4 (over z).
Axes of the slice: x: 2, y: 2, z: 4, core: 2. Of those that a mesh axis runs over, the one named last changes fastest.
Arguments:
- queries: bfloat16 [384, 2048], P('seq', 'tp'), may hold values from -16 to 16
- keys: bfloat16 [384, 2048], P('seq', 'tp'), may hold values from -16 to 16
- values: bfloat16 [384, 2048], P('seq', 'tp'), may hold values from -6 to 6
- patch_stream: bfloat16 [384, 4096], P('seq', 'tp'), may hold values from -6 to 6
- out_weight: bfloat16 [2048, 4096], P('tp', 'seq'), may hold values from -1 to 1
- down_weight: bfloat16 [4096, 1280], P('tp'), may hold values from -0.09375 to 0.09375
- byte_states: bfloat16 [1536, 1280], P('seq', 'tp'), may hold values from -6 to 6
- patch_starts: int32 [8, 48], P('seq'), may hold values from 0 to 192, as said below
Outputs:
- new_patches: bfloat16 [384, 4096], P('seq', 'tp')
- new_bytes: bfloat16 [1536, 1280], P('seq', 'tp')
Inputs may be any that keep to these rules, and one draw needn't show every extreme that they name: `patch_starts`: each row d lists rising offsets within device d's 192 bytes at which patches start: the first is 0 in row 0 and from 4 to 7 in the other rows, the others are 8 or more; at least 24 entries of a row are offsets, some row has all 48, and the remaining entries at the end of a row equal 192.
All inputs are finite; a program needn't handle non-finite values.
Results may differ from a plain program's by a relative error of at most 0.015.
Values may be sent and summed in bfloat16 or wider, within the bound.
A program may use at most 128 MiB of HBM per device.

v0:
```python
import jax
import jax.numpy as jnp
from jax import lax
from jax.sharding import PartitionSpec as P

DH = 128
B_DEV = 192


NEG = -1e30


def from_behind(value, axis, by):
    devices = lax.axis_size(axis)
    pairs = [(i, i + by) for i in range(devices) if 0 <= i + by < devices]
    return lax.ppermute(value, axis, pairs)


def on_device(
    queries, keys, values, patch_stream, out_weight, down_weight, byte_states, patch_starts
):
    rows = queries.shape[0]
    width = queries.shape[1]
    heads = width // DH
    scale = DH ** (-0.5)
    starts_row = patch_starts.reshape(-1)
    valid = starts_row < B_DEV
    key_mask = valid.astype(jnp.bfloat16)
    first_slot = lax.axis_index("seq") * rows
    query_ids = first_slot + jnp.arange(rows, dtype=jnp.int32)
    query_heads = queries.reshape(rows, heads, DH)
    peak = jnp.full((heads, rows), NEG, jnp.float32)
    key_piece = lax.all_gather(keys, "seq", axis=0, tiled=True)
    value_piece = lax.all_gather(values, "seq", axis=0, tiled=True)
    mask_piece = lax.all_gather(key_mask, "seq", axis=0, tiled=True)
    count = key_piece.shape[0]
    key_heads = key_piece.reshape(count, heads, DH)
    value_heads = value_piece.reshape(count, heads, DH)
    scores = (
        jnp.einsum("qhd,khd->hqk", query_heads, key_heads, preferred_element_type=jnp.float32)
        * scale
    )
    key_ids = jnp.arange(count, dtype=jnp.int32)
    allowed = (mask_piece > 0)[None, :] & (key_ids[None, :] <= query_ids[:, None])
    scores = jnp.where(allowed[None], scores, NEG)
    new_peak = jnp.maximum(peak, jnp.max(scores, axis=-1))
    expo = jnp.exp(scores - new_peak[:, :, None])
    total = jnp.sum(expo, axis=-1)
    weights = expo.astype(jnp.bfloat16)
    summed = jnp.einsum("hqk,khd->hqd", weights, value_heads, preferred_element_type=jnp.float32)
    peak, total, summed = (new_peak, total, summed)
    attn = summed / total[:, :, None]
    attn = jnp.transpose(attn, (1, 0, 2)).reshape(rows, width).astype(jnp.bfloat16)
    partial_value = jnp.dot(
        attn,
        lax.all_gather(out_weight, "seq", axis=1, tiled=True),
        preferred_element_type=jnp.float32,
    )
    mixed = lax.psum_scatter(
        partial_value.astype(jnp.bfloat16), "tp", scatter_dimension=1, tiled=True
    ).astype(jnp.float32)
    new_patches = (patch_stream.astype(jnp.float32) + mixed).astype(jnp.bfloat16)
    down_terms = jnp.dot(new_patches, down_weight, preferred_element_type=jnp.float32)
    patch_down = lax.psum_scatter(
        down_terms.astype(jnp.bfloat16), "tp", scatter_dimension=1, tiled=True
    )
    following = jnp.concatenate([valid[1:], jnp.zeros((1,), jnp.bool_)])
    last_pick = (valid & jnp.logical_not(following)).astype(jnp.bfloat16)[None, :]
    last_state = jnp.dot(last_pick, patch_down, preferred_element_type=jnp.float32).astype(
        jnp.bfloat16
    )
    earlier_state = from_behind(last_state, "seq", 1)
    position = jnp.arange(B_DEV, dtype=jnp.int32)
    ends = jnp.concatenate([starts_row[1:], jnp.full((1,), B_DEV, jnp.int32)])
    member = (starts_row[None, :] <= position[:, None]) & (position[:, None] < ends[None, :])
    member = member.astype(jnp.bfloat16)
    before = (position < starts_row[0]).astype(jnp.float32)[:, None]
    added = jnp.dot(member, patch_down, preferred_element_type=jnp.float32)
    added = added + before * earlier_state.astype(jnp.float32)
    new_bytes = (byte_states.astype(jnp.float32) + added).astype(jnp.bfloat16)
    return (new_patches, new_bytes)


def solution(mesh):
    in_specs = (
        P("seq", "tp"),
        P("seq", "tp"),
        P("seq", "tp"),
        P("seq", "tp"),
        P("tp", "seq"),
        P("tp", None),
        P("seq", "tp"),
        P("seq", None),
    )
    out_specs = (P("seq", "tp"), P("seq", "tp"))
    return jax.shard_map(
        on_device, mesh=mesh, in_specs=in_specs, out_specs=out_specs, check_vma=False
    )
```

profile of v0, /device:TPU:4, one launch (start us, length us, event | category | flops | bytes accessed | tf_op | source)
XLA Modules:
  0.0 111.4 jit_solution(1942198980540174609)
XLA Ops:
  7.2 0.7 all-gather.2.cloned.1.call-update
  8.0 9.6 %all_gather.13 = bf16[384,512]{1,0:T(8,128)(2,1)S(1)} all-gather(bf16[48,512]{1,0:T(8,128)(2,1)} %param.9), channel_id=1, replica_groups=mesh['seq'=8,'tp'=4] {'seq'}, dimensions={0}, use_global_device_ids=true | all-gather | bytes 442368 | tf_op jit(solution)/shard_map/all_gather | solution.py:33
  17.5 0.2 copy.17
  17.8 11.0 %all_gather.14 = bf16[384,512]{1,0:T(8,128)(2,1)S(1)} all-gather(bf16[48,512]{1,0:T(8,128)(2,1)} %param.10), channel_id=1, replica_groups=mesh['seq'=8,'tp'=4] {'seq'}, dimensions={0}, use_global_device_ids=true | all-gather | bytes 442368 | tf_op jit(solution)/shard_map/all_gather | solution.py:34
  28.8 0.9 copy.20
  29.7 1.2 %dynamic-slice = u32[1]{0:T(128)} dynamic-slice(u32[32]{0:T(128)} %constant.29, u32[]{:T(128)S(6)} %add.28), dynamic_slice_sizes={1} | dynamic-slice | bytes 12
  31.6 0.7 broadcast_compare_fusion.1
  32.3 0.2 dynamic-update-slice
  32.5 14.2 %all-reduce = bf16[384]{0:T(512)(128)(2,1)S(1)} all-reduce(bf16[384]{0:T(512)(128)(2,1)S(1)} %dynamic-update-slice), channel_id=1, replica_groups=mesh['seq'=8,'tp'=4] {'seq'}, use_global_device_ids=true, to_apply=%add | all-reduce | flops 384 | bytes 1536
  46.6 0.1 fusion.15
  46.7 1.1 fusion.29
  47.8 0.2 fusion.4
  48.0 1.3 %fusion.3 = bf16[4,6,8,128]{3,2,1,0:T(8,128)(2,1)S(1)} fusion(bf16[384,4,128]{0,2,1:T(8,128)(2,1)} %bitcast.53, f32[4,48,384]{2,1,0:T(8,128)S(1)} %get-tuple-element.5, f32[4,48]{1,0:T(4,128)S(1)} %broadcast_maximum_fusion, f32[48,4]{0,1:T(4,128)S(1)} %bitcast.54), kind=kOutput, calls=%fused_computation.7 | convolution fusion | flops 19070976 | bytes 738816 | tf_op jit(solution)/shard_map/hqk,khd->hqd/dot_general | solution.py:50
  49.4 0.2 all-gather.2.cloned.1.call-done
  49.6 3.8 %convolution_convert_fusion = bf16[48,4096]{1,0:T(8,128)(2,1)} fusion(bf16[512,4096]{1,0:T(8,128)(2,1)} %all-gather.2.cloned.1.call-done, bf16[4,6,8,128]{3,2,1,0:T(8,128)(2,1)S(1)} %fusion.3), kind=kOutput, calls=%fused_computation | convolution fusion | flops 201523200 | bytes 4636672 | tf_op jit(solution)/shard_map/dot_general | solution.py:54
  53.5 21.3 %reduce-scatter.5.cloned.1.call-done = bf16[48,1024]{1,0:T(8,128)(2,1)} async-done(((bf16[48,4096]{1,0:T(8,128)(2,1)}), bf16[48,1024]{1,0:T(8,128)(2,1)}) %reduce-scatter.5.cloned.1.call-update) | async-done | bytes 98320 | tf_op jit(solution)/shard_map/reduce_scatter | solution.py:59
  74.8 0.9 add_convert_fusion.1
  75.8 0.6 convolution_convert_fusion.1
  76.4 0.9 copy.25
  77.4 18.8 %reduce-scatter.7.cloned.1.call-done = bf16[320,48]{1,0:T(8,128)(2,1)} async-done(((bf16[1280,48]{1,0:T(8,128)(2,1)}), bf16[320,48]{1,0:T(8,128)(2,1)}) %reduce-scatter.7.cloned.1.call-update) | async-done | bytes 30736
  96.2 1.1 convolution_reduce_fusion
  97.3 1.9 %collective-permute-start = (bf16[1,320]{1,0:T(2,128)(2,1)S(1)}, bf16[1,320]{1,0:T(2,128)(2,1)S(1)}, u32[]{:S(2)}, u32[]{:S(2)}) collective-permute-start(bf16[1,320]{1,0:T(2,128)(2,1)S(1)} %convert_element_type.61), channel_id=1, source_target_pairs={{0,4},{4,8},{8,12},{12,16},{16,20},{20,24},{24,28},{1,5},{5,9},{9,... | collective-permute-start | bytes 1928 | tf_op jit(solution)/shard_map/ppermute | solution.py:16
  99.3 3.8 %collective-permute-done = bf16[1,320]{1,0:T(2,128)(2,1)S(1)} collective-permute-done((bf16[1,320]{1,0:T(2,128)(2,1)S(1)}, bf16[1,320]{1,0:T(2,128)(2,1)S(1)}, u32[]{:S(2)}, u32[]{:S(2)}) %collective-permute-start) | collective-permute-done | bytes 672 | tf_op jit(solution)/shard_map/ppermute | solution.py:16
  103.1 1.8 %add_convert_fusion = bf16[192,320]{1,0:T(8,128)(2,1)} fusion(bf16[192,320]{1,0:T(8,128)(2,1)S(1)} %copy-done.4, f32[320]{0:T(512)S(1)} %convert_reduce_fusion, f32[192]{0:T(256)S(1)} %compare_convert_fusion, bf16[320,48]{1,0:T(8,128)(2,1)} %reduce-scatter.7.cloned.1.call-done, s32[48]{0:T(128)S(1)} %pad_add_fusion, s32[48]{0:T(128)S(1)} %bitcast.56), kind=kOutput, calls=%fused_computation.9 | convolution fusion | flops 6233088 | bytes 278912 | tf_op jit(solution)/shard_map/dot_general | solution.py:78
  (25 shorter events, 0.5 us)
Async XLA Ops:
  7.2 68.6 %copy-start = (bf16[1024,1280]{1,0:T(8,128)(2,1)S(1)}, bf16[1024,1280]{1,0:T(8,128)(2,1)}, u32[]{:S(2)}) copy-start(bf16[1024,1280]{1,0:T(8,128)(2,1)} %param.13) | copy-start | bytes 7864324
  7.2 42.4 %all-gather.2.cloned.1.call-start = ((), (), s32[]{:S(2)}) async-start(), calls=%async_computation.2 | async-start | bytes 4718592 | tf_op jit(solution)/shard_map/all_gather | solution.py:56
  7.9 66.9 %reduce-scatter.5.cloned.1.call-start = ((), (), s32[]{:S(2)}) async-start(), calls=%async_computation.3 | async-start | bytes 491520 | tf_op jit(solution)/shard_map/reduce_scatter | solution.py:59
  17.7 35.7 %copy-start.3 = (s32[1,48]{1,0:T(1,128)S(1)}, s32[1,48]{1,0:T(1,128)}, u32[]{:S(2)}) copy-start(s32[1,48]{1,0:T(1,128)} %param.15) | copy-start | bytes 580
  17.8 57.1 %copy-start.2 = (bf16[48,1024]{1,0:T(8,128)(2,1)S(1)}, bf16[48,1024]{1,0:T(8,128)(2,1)}, u32[]{:S(2)}) copy-start(bf16[48,1024]{1,0:T(8,128)(2,1)} %param.11) | copy-start | bytes 294916
  49.4 53.8 %copy-start.4 = (bf16[192,320]{1,0:T(8,128)(2,1)S(1)}, bf16[192,320]{1,0:T(8,128)(2,1)}, u32[]{:S(2)}) copy-start(bf16[192,320]{1,0:T(8,128)(2,1)} %param.14) | copy-start | bytes 368644
  53.4 42.8 %reduce-scatter.7.cloned.1.call-start = ((), (), s32[]{:S(2)}) async-start(), calls=%async_computation.4 | async-start | bytes 409600
  75.8 29.1 %copy-start.1 = (bf16[48,1024]{1,0:T(8,128)(2,1)}, bf16[48,1024]{1,0:T(8,128)(2,1)S(1)}, u32[]{:S(2)}) copy-start(bf16[48,1024]{1,0:T(8,128)(2,1)S(1)} %add_convert_fusion.1) | copy-start | bytes 294916
  97.3 5.8 %collective-permute-start = (bf16[1,320]{1,0:T(2,128)(2,1)S(1)}, bf16[1,320]{1,0:T(2,128)(2,1)S(1)}, u32[]{:S(2)}, u32[]{:S(2)}) collective-permute-start(bf16[1,320]{1,0:T(2,128)(2,1)S(1)} %convert_element_type.61), channel_id=1, source_target_pairs={{0,4},{4,8},{8,12},{12,16},{16,20},{20,24},{24,28},{1,5},{5,9},{9,... | collective-permute-start | bytes 1928 | tf_op jit(solution)/shard_map/ppermute | solution.py:16
Sparse Core Ops, SparseCore 0:
  9.9 39.6 all-gather.1
  53.5 21.2 reduce-scatter.4
  77.4 18.7 reduce-scatter.6
where the time goes:
time: 112 us; the launch traced here: 111 us
  waiting for transfers between devices  44.8 us (40%)
  blocking collectives  34.7 us (31%)
  between operations  14.5 us (13%)
  matrix products  9.62 us (9%)
  local copies, waits for them, and re-layouts  3.66 us (3%)
  starting transfers between devices  2.04 us (2%)
  other arithmetic  2.02 us (2%)
    reduce_scatter x1, waiting for transfers between devices, on_device(): lax.psum_scatter(partial_value.astype(jnp.bfloat16), 'tp', scatter_dimens...  21.3 us
    unnamed x4, waiting for transfers between devices  19.5 us
    unnamed x1, blocking collectives  14.2 us
    all_gather x1, blocking collectives, on_device(): value_piece = lax.all_gather(values, 'seq', axis=0, tiled=True)  11 us
    all_gather x1, blocking collectives, on_device(): key_piece = lax.all_gather(keys, 'seq', axis=0, tiled=True)  9.56 us
    ppermute x1, waiting for transfers between devices, from_behind(): return lax.ppermute(value, axis, pairs)  3.79 us
    dot_general x1, matrix products, on_device(): jnp.dot(attn, lax.all_gather(out_weight, 'seq', axis=1, tiled=True), pref...  3.78 us
    unnamed x14, local copies, waits for them, and re-layouts  2.37 us
  transfers between devices with their start and end apart: 4, of which 4 were waited for; matrix products, arithmetic and copies ran while one was open for 6% of the time, Pallas kernels for 0%

commit v1 on v0

--- a/solution.py
+++ b/solution.py
@@ -1,6 +1,10 @@
+import functools
+
 import jax
 import jax.numpy as jnp
 from jax import lax
+from jax.experimental import pallas as pl
+from jax.experimental.pallas import tpu as pltpu
 from jax.sharding import PartitionSpec as P
 
 DH = 128
@@ -16,7 +20,7 @@
     return lax.ppermute(value, axis, pairs)
 
 
-def on_device(
+def plain_form(
     queries, keys, values, patch_stream, out_weight, down_weight, byte_states, patch_starts
 ):
     rows = queries.shape[0]
@@ -81,6 +85,314 @@
     return (new_patches, new_bytes)
 
 
+MESH = pl.DeviceIdType.MESH
+
+
+def fused_kernel(
+    sizes,
+    q_hbm, k_hbm, v_hbm, ps_hbm, ow_hbm, dw_hbm, bs_hbm, st_ref,
+    np_hbm, nb_hbm,
+    qbuf, kbuf, vbuf, sbuf, aown, abuf, cbuf, rbuf, npbuf, dsend, dbuf, lsend, lbuf,
+    ow, dw, ps, bs, pd, nb,
+    qs, qr, ks, kr, vs, vr, ss, sr, as_, ar, cs, cr, ds_, dr, ls, lr, loc,
+):
+    S, T, H, rows, local = sizes
+    G = S // H
+    CP = S // T
+    cols = ow.shape[1]
+    me = lax.axis_index("seq")
+    z = lax.axis_index("tp")
+    head = me // G
+    g = lax.rem(me, G)
+
+    loads = [
+        pltpu.make_async_copy(src, dst, loc.at[n])
+        for n, (src, dst) in enumerate(
+            ((ow_hbm, ow), (ps_hbm, ps), (dw_hbm, dw), (bs_hbm, bs))
+        )
+    ]
+    for load in loads:
+        load.start()
+
+    starts = jnp.broadcast_to(st_ref[...], (8, rows))
+    valid8 = jnp.where(starts < B_DEV, 1.0, 0.0)
+    sbuf[me] = valid8
+
+    barrier = pltpu.get_barrier_semaphore()
+    for i in range(S):
+        for t in range(T):
+            if i or t:
+                pl.semaphore_signal(
+                    barrier, inc=1,
+                    device_id={"seq": lax.rem(me + i, S), "tp": lax.rem(z + t, T)},
+                    device_id_type=MESH,
+                )
+    pl.semaphore_wait(barrier, S * T - 1)
+
+    def lanes(block, width):
+        return pl.ds(pl.multiple_of(block * width, 128), width)
+
+    sends = []
+
+    def send(src, dst, ssem, rsem, seq, tp):
+        copy = pltpu.make_async_remote_copy(
+            src_ref=src, dst_ref=dst, send_sem=ssem, recv_sem=rsem,
+            device_id={"seq": seq, "tp": tp}, device_id_type=MESH,
+        )
+        copy.start()
+        sends.append(copy)
+
+    def arrived(dst, sem):
+        pltpu.make_async_copy(dst, dst, sem).wait()
+
+    for i in range(S):
+        tgt = lax.rem(me + i, S)
+        part = lanes(tgt // G, DH)
+        if i == 0:
+            pltpu.make_async_copy(k_hbm.at[:, part], kbuf.at[me], kr.at[me]).start()
+            pltpu.make_async_copy(v_hbm.at[:, part], vbuf.at[me], vr.at[me]).start()
+            pltpu.make_async_copy(q_hbm.at[:, part], qbuf.at[head], qr.at[head]).start()
+        else:
+            send(k_hbm.at[:, part], kbuf.at[me], ks.at[i], kr.at[me], tgt, z)
+            if i % G == 0:
+                send(q_hbm.at[:, part], qbuf.at[head], qs.at[i], qr.at[head], tgt, z)
+            send(sbuf.at[me], sbuf.at[me], ss.at[i], sr.at[me], tgt, z)
+            send(v_hbm.at[:, part], vbuf.at[me], vs.at[i], vr.at[me], tgt, z)
+
+    count = S * rows
+    key_row = lax.broadcasted_iota(jnp.int32, (rows, count), 1)
+    slot = lax.broadcasted_iota(jnp.int32, (rows, count), 0)
+    spread = key_row == slot
+    for d in range(1, S):
+        spread = spread | (key_row == slot + d * rows)
+    spread = jnp.where(spread, 1.0, 0.0).astype(jnp.bfloat16)
+
+    for i in range(1, S):
+        src = lax.rem(me + i, S)
+        arrived(sbuf.at[src], sr.at[src])
+    which = lax.broadcasted_iota(jnp.int32, (S, rows), 0)
+    valid = jnp.zeros((S, rows), jnp.float32)
+    for d in range(S):
+        valid = jnp.where(which == d, sbuf[d][:1, :], valid)
+    laid = jnp.dot(valid.astype(jnp.bfloat16), spread, preferred_element_type=jnp.float32)
+    owner = lax.broadcasted_iota(jnp.int32, (S, count), 0) * rows
+    lane = lax.broadcasted_iota(jnp.int32, (S, count), 1)
+    laid = jnp.where((lane >= owner) & (lane < owner + rows), laid, 0.0)
+    key_valid = jnp.sum(laid, axis=0, keepdims=True)
+
+    mine = H * rows
+    row = lax.broadcasted_iota(jnp.int32, (mine, count), 0)
+    block = jnp.zeros((mine, count), jnp.int32)
+    for j in range(1, H):
+        block = block + jnp.where(row >= j * rows, (G - 1) * rows, 0)
+    query = row + block + g * rows
+    key = lax.broadcasted_iota(jnp.int32, (mine, count), 1)
+    allowed = (key <= query) & (key_valid > 0.0)
+
+    for j in range(H):
+        arrived(qbuf.at[j], qr.at[j])
+    for d in range(S):
+        arrived(kbuf.at[d], kr.at[d])
+    scores = lax.dot_general(
+        qbuf[...].reshape(mine, DH), kbuf[...].reshape(count, DH),
+        (((1,), (1,)), ((), ())), preferred_element_type=jnp.float32,
+    ) * (DH ** -0.5)
+    scores = jnp.where(allowed, scores, NEG)
+    peak = jnp.max(scores, axis=1, keepdims=True)
+    expo = jnp.exp(scores - peak)
+    total = jnp.sum(expo, axis=1, keepdims=True)
+    for d in range(S):
+        arrived(vbuf.at[d], vr.at[d])
+    summed = jnp.dot(
+        expo.astype(jnp.bfloat16), vbuf[...].reshape(count, DH),
+        preferred_element_type=jnp.float32,
+    )
+    aown[...] = (summed / total).astype(jnp.bfloat16).reshape(H, rows, DH)
+
+    for e in range(G):
+        for jj in range(H):
+            i = jj * G + e
+            tgt = lax.rem(me + i, S)
+            dst = abuf.at[g, :, :, lanes(head, DH)]
+            if i == 0:
+                pltpu.make_async_copy(aown, dst, ar.at[me]).start()
+            else:
+                send(aown, dst, as_.at[i], ar.at[me], tgt, z)
+    loads[0].wait()
+
+    chunk = me // CP
+    place = lax.rem(me, CP)
+    for e in range(G):
+        gg = lax.rem(g + e, G)
+        for jj in range(H):
+            src = lax.rem(head + jj, H) * G + gg
+            arrived(aown, ar.at[src])
+        product = jnp.dot(
+            abuf[gg].reshape(mine, H * DH), ow[...], preferred_element_type=jnp.float32
+        )
+        cbuf[gg] = product.astype(jnp.bfloat16).reshape(H, rows, cols)
+        for jj in range(H):
+            j = lax.rem(head + jj, H)
+            tgt = j * G + gg
+            n = e * H + jj
+            out = pltpu.make_async_remote_copy(
+                src_ref=cbuf.at[gg, j], dst_ref=rbuf.at[z, place],
+                send_sem=cs.at[n], recv_sem=cr.at[z, place],
+                device_id={"seq": tgt, "tp": chunk}, device_id_type=MESH,
+            )
+            if n == 0:
+                home = chunk == z
+
+                @pl.when(home)
+                def _():
+                    pltpu.make_async_copy(
+                        cbuf.at[gg, j], rbuf.at[z, place], cr.at[z, place]
+                    ).start()
+
+                @pl.when(jnp.logical_not(home))
+                def _():
+                    out.start()
+
+                first_out = out
+            else:
+                out.start()
+                sends.append(out)
+
+    loads[1].wait()
+    for t in range(T):
+        for p in range(CP):
+            arrived(rbuf.at[t, p], cr.at[t, p])
+    for p in range(CP):
+        mixed = rbuf[0, p].astype(jnp.float32)
+        for t in range(1, T):
+            mixed = mixed + rbuf[t, p].astype(jnp.float32)
+        at = pl.ds(p * cols, cols)
+        npbuf[:, at] = (ps[:, at].astype(jnp.float32) + mixed).astype(jnp.bfloat16)
+    np_out = pltpu.make_async_copy(npbuf, np_hbm, loc.at[4])
+    np_out.start()
+
+    loads[2].wait()
+    wide = dw.shape[1]
+    padded = dbuf.shape[2]
+    down = jnp.dot(npbuf[...], dw[...], preferred_element_type=jnp.float32)
+
+    def share(x, t):
+        turned = x if t == 0 else pltpu.roll(x, wide - t * local, 1)
+        return turned[:, :padded].astype(jnp.bfloat16)
+
+    for t in range(T):
+        dsend[t] = share(down, t)
+    for i in range(1, T):
+        t = lax.rem(z + i, T)
+        send(dsend.at[t], dbuf.at[z], ds_.at[i], dr.at[z], me, t)
+    dbuf[z] = dsend[z]
+
+    held = jnp.sum(valid8[:1, :], axis=1, keepdims=True)
+    lane16 = lax.broadcasted_iota(jnp.int32, (16, rows), 1).astype(jnp.float32)
+    pick = jnp.where(lane16 == held - 1.0, 1.0, 0.0).astype(jnp.bfloat16)
+    last = jnp.dot(pick, down.astype(jnp.bfloat16), preferred_element_type=jnp.float32)
+    for t in range(T):
+        lsend[t] = share(last, t)
+    after = lax.rem(me + 1, S)
+    for i in range(T):
+        t = lax.rem(z + i, T)
+        send(lsend.at[t], lbuf.at[z], ls.at[i], lr.at[z], after, t)
+
+    position = lax.broadcasted_iota(jnp.int32, (B_DEV, rows), 0)
+    begun = jnp.where(st_ref[...] <= position, 1.0, 0.0)
+    reached = jnp.sum(begun, axis=1, keepdims=True)
+    lane_b = lax.broadcasted_iota(jnp.int32, (B_DEV, rows), 1).astype(jnp.float32)
+    member = jnp.where(lane_b == reached - 1.0, 1.0, 0.0).astype(jnp.bfloat16)
+    before = reached < 0.5
+    loads[3].wait()
+
+    for i in range(1, T):
+        t = lax.rem(z + i, T)
+        arrived(dbuf.at[t], dr.at[t])
+    for t in range(T):
+        arrived(lbuf.at[t], lr.at[t])
+    state = dbuf[0].astype(jnp.float32)
+    earlier = lbuf[0].astype(jnp.float32)
+    for t in range(1, T):
+        state = state + dbuf[t].astype(jnp.float32)
+        earlier = earlier + lbuf[t].astype(jnp.float32)
+    state = state.astype(jnp.bfloat16)
+    earlier = earlier.astype(jnp.bfloat16).astype(jnp.float32)[:1, :]
+    added = jnp.dot(member, state, preferred_element_type=jnp.float32)
+    pd[...] = jnp.where(before, earlier, added)
+    nb[...] = (bs[...].astype(jnp.float32) + pd[:, :local]).astype(jnp.bfloat16)
+    nb_out = pltpu.make_async_copy(nb, nb_hbm, loc.at[5])
+    nb_out.start()
+
+    for copy in sends:
+        copy.wait_send()
+
+    @pl.when(jnp.logical_not(home))
+    def _():
+        first_out.wait_send()
+
+    np_out.wait()
+    nb_out.wait()
+
+
+def fused_form(
+    S, T, queries, keys, values, patch_stream, out_weight, down_weight, byte_states, patch_starts
+):
+    rows, width = queries.shape
+    H = width // DH
+    G = S // H
+    cols = out_weight.shape[1]
+    bytes_here, local = byte_states.shape
+    padded = -(-local // 128) * 128
+    bf = jnp.bfloat16
+    sem = pltpu.SemaphoreType.DMA
+    scratch = [
+        pltpu.VMEM((H, rows, DH), bf),
+        pltpu.VMEM((S, rows, DH), bf),
+        pltpu.VMEM((S, rows, DH), bf),
+        pltpu.VMEM((S, 8, rows), jnp.float32),
+        pltpu.VMEM((H, rows, DH), bf),
+        pltpu.VMEM((G, H, rows, width), bf),
+        pltpu.VMEM((G, H, rows, cols), bf),
+        pltpu.VMEM((T, S // T, rows, cols), bf),
+        pltpu.VMEM(patch_stream.shape, bf),
+        pltpu.VMEM((T, rows, padded), bf),
+        pltpu.VMEM((T, rows, padded), bf),
+        pltpu.VMEM((T, 16, padded), bf),
+        pltpu.VMEM((T, 16, padded), bf),
+        pltpu.VMEM(out_weight.shape, bf),
+        pltpu.VMEM(down_weight.shape, bf),
+        pltpu.VMEM(patch_stream.shape, bf),
+        pltpu.VMEM(byte_states.shape, bf),
+        pltpu.VMEM((bytes_here, padded), jnp.float32),
+        pltpu.VMEM(byte_states.shape, bf),
+        sem((S,)), sem((H,)), sem((S,)), sem((S,)), sem((S,)), sem((S,)),
+        sem((S,)), sem((S,)), sem((S,)), sem((S,)), sem((S,)), sem((T, S // T)),
+        sem((T,)), sem((T,)), sem((T,)), sem((T,)), sem((6,)),
+    ]
+    hbm = pl.BlockSpec(memory_space=pl.ANY)
+    return tuple(pl.pallas_call(
+        functools.partial(fused_kernel, (S, T, H, rows, local)),
+        out_shape=(
+            jax.ShapeDtypeStruct(patch_stream.shape, bf),
+            jax.ShapeDtypeStruct(byte_states.shape, bf),
+        ),
+        in_specs=[hbm] * 7 + [pl.BlockSpec(memory_space=pltpu.VMEM)],
+        out_specs=(hbm, hbm),
+        scratch_shapes=scratch,
+        compiler_params=pltpu.CompilerParams(collective_id=0, has_side_effects=True),
+    )(queries, keys, values, patch_stream, out_weight, down_weight, byte_states, patch_starts))
+
+
+def on_device(S, T, *args):
+    queries, out_weight = args[0], args[4]
+    heads = queries.shape[1] // DH
+    aligned = out_weight.shape[1] % 128 == 0 and queries.shape[0] % 16 == 0
+    if aligned and S % heads == 0 and S % T == 0 and S >= T:
+        return fused_form(S, T, *args)
+    return plain_form(*args)
+
+
 def solution(mesh):
     in_specs = (
         P("seq", "tp"),
@@ -94,5 +406,6 @@
     )
     out_specs = (P("seq", "tp"), P("seq", "tp"))
     return jax.shard_map(
-        on_device, mesh=mesh, in_specs=in_specs, out_specs=out_specs, check_vma=False
-    )
+        functools.partial(on_device, mesh.shape["seq"], mesh.shape["tp"]),
+        mesh=mesh, in_specs=in_specs, out_specs=out_specs, check_vma=False
+    )

time: 112 us -> 55.7 us (0.50)
  the two profiles are of different devices: /device:TPU:4 before, /device:TPU:0 now
where the time goes in v1:
time: 55.7 us; the launch traced here: 55.1 us
  Pallas kernels  51.3 us (92%)
  local copies, waits for them, and re-layouts  3.12 us (6%)
  between operations  0.64 us (1%)
    pallas_call x1, Pallas kernels, fused_form(): pl.pallas_call(functools.partial(fused_kernel, (S, T, H, rows, local)), o...  51.3 us
    unnamed x2, local copies, waits for them, and re-layouts  3.12 us

profile of v1, /device:TPU:0, one launch (start us, length us, event | category | flops | bytes accessed | tf_op | source)
XLA Modules:
  0.0 55.1 jit_solution(10405182573366334432)
XLA Ops:
  0.6 51.3 %shard_map.95 = (bf16[48,1024]{1,0:T(8,128)(2,1)}, bf16[192,320]{1,0:T(8,128)(2,1)}) custom-call(bf16[48,512]{1,0:T(8,128)(2,1)} %q_hbm.1, bf16[48,512]{1,0:T(8,128)(2,1)} %k_hbm.1, bf16[48,512]{1,0:T(8,128)(2,1)} %v_hbm.1, bf16[48,1024]{1,0:T(8,128)(2,1)} %ps_hbm.1, bf16[512,512]{1,0:T(8,128)(2,1)} %ow_hbm.1, bf16[1024,1280]{1,0:T(8,128)(2,1)} %dw_hbm.1, ...), custom_call_target="tpu_custom_call" | custom-call | tf_op jit(solution)/shard_map/pallas_call | solution.py:374
  51.9 1.5 %copy.12 = bf16[48,1024]{1,0:T(8,128)(2,1)} copy(bf16[48,1024]{1,0:T(8,128)(2,1)} %get-tuple-element.4) | data formatting | bytes 196608
  53.5 1.6 %copy.13 = bf16[192,320]{1,0:T(8,128)(2,1)} copy(bf16[192,320]{1,0:T(8,128)(2,1)} %get-tuple-element.5) | data formatting | bytes 245760

commit v2 on v1

--- a/solution.py
+++ b/solution.py
@@ -92,9 +92,9 @@
     sizes,
     q_hbm, k_hbm, v_hbm, ps_hbm, ow_hbm, dw_hbm, bs_hbm, st_ref,
     np_hbm, nb_hbm,
-    qbuf, kbuf, vbuf, sbuf, aown, abuf, cbuf, rbuf, npbuf, dsend, dbuf, lsend, lbuf,
+    qbuf, kbuf, vbuf, sbuf, aown, abuf, cbuf, rel, rbuf, npbuf, dsend, dbuf, lsend, lbuf,
     ow, dw, ps, bs, pd, nb,
-    qs, qr, ks, kr, vs, vr, ss, sr, as_, ar, cs, cr, ds_, dr, ls, lr, loc,
+    qs, qr, ks, kr, vs, vr, ss, sr, as_, ar, cs, relr, fs, cr, ds_, dr, ls, lr, loc,
 ):
     S, T, H, rows, local = sizes
     G = S // H
@@ -119,15 +119,15 @@
     sbuf[me] = valid8
 
     barrier = pltpu.get_barrier_semaphore()
-    for i in range(S):
-        for t in range(T):
-            if i or t:
-                pl.semaphore_signal(
-                    barrier, inc=1,
-                    device_id={"seq": lax.rem(me + i, S), "tp": lax.rem(z + t, T)},
-                    device_id_type=MESH,
-                )
-    pl.semaphore_wait(barrier, S * T - 1)
+    for i in range(1, S):
+        pl.semaphore_signal(
+            barrier, inc=1, device_id={"seq": lax.rem(me + i, S), "tp": z}, device_id_type=MESH
+        )
+    for i in range(1, T):
+        pl.semaphore_signal(
+            barrier, inc=1, device_id={"seq": me, "tp": lax.rem(z + i, T)}, device_id_type=MESH
+        )
+    pl.semaphore_wait(barrier, S + T - 2)
 
     def lanes(block, width):
         return pl.ds(pl.multiple_of(block * width, 128), width)
@@ -220,8 +220,6 @@
                 send(aown, dst, as_.at[i], ar.at[me], tgt, z)
     loads[0].wait()
 
-    chunk = me // CP
-    place = lax.rem(me, CP)
     for e in range(G):
         gg = lax.rem(g + e, G)
         for jj in range(H):
@@ -234,29 +232,30 @@
         for jj in range(H):
             j = lax.rem(head + jj, H)
             tgt = j * G + gg
-            n = e * H + jj
-            out = pltpu.make_async_remote_copy(
-                src_ref=cbuf.at[gg, j], dst_ref=rbuf.at[z, place],
-                send_sem=cs.at[n], recv_sem=cr.at[z, place],
-                device_id={"seq": tgt, "tp": chunk}, device_id_type=MESH,
+            if e == 0 and jj == 0:
+                pltpu.make_async_copy(cbuf.at[gg, j], rel.at[me], relr.at[me]).start()
+            else:
+                send(cbuf.at[gg, j], rel.at[me], cs.at[e * H + jj], relr.at[me], tgt, z)
+
+    passed = []
+    for e in range(G):
+        for jj in range(H):
+            src = lax.rem(head - jj + H, H) * G + lax.rem(g - e + G, G)
+            chunk, place = src // CP, lax.rem(src, CP)
+            arrived(rel.at[src], relr.at[src])
+            dst, dsem = rbuf.at[z, place], cr.at[z, place]
+            onward = pltpu.make_async_remote_copy(
+                src_ref=rel.at[src], dst_ref=dst, send_sem=fs.at[e * H + jj], recv_sem=dsem,
+                device_id={"seq": me, "tp": chunk}, device_id_type=MESH,
             )
-            if n == 0:
-                home = chunk == z
-
-                @pl.when(home)
-                def _():
-                    pltpu.make_async_copy(
-                        cbuf.at[gg, j], rbuf.at[z, place], cr.at[z, place]
-                    ).start()
-
-                @pl.when(jnp.logical_not(home))
-                def _():
-                    out.start()
-
-                first_out = out
-            else:
-                out.start()
-                sends.append(out)
+            away = chunk != z
+            pl.when(away)(onward.start)
+
+            @pl.when(jnp.logical_not(away))
+            def _():
+                pltpu.make_async_copy(rel.at[src], dst, dsem).start()
+
+            passed.append((away, onward))
 
     loads[1].wait()
     for t in range(T):
@@ -327,9 +326,8 @@
     for copy in sends:
         copy.wait_send()
 
-    @pl.when(jnp.logical_not(home))
-    def _():
-        first_out.wait_send()
+    for away, onward in passed:
+        pl.when(away)(onward.wait_send)
 
     np_out.wait()
     nb_out.wait()
@@ -354,6 +352,7 @@
         pltpu.VMEM((H, rows, DH), bf),
         pltpu.VMEM((G, H, rows, width), bf),
         pltpu.VMEM((G, H, rows, cols), bf),
+        pltpu.VMEM((S, rows, cols), bf),
         pltpu.VMEM((T, S // T, rows, cols), bf),
         pltpu.VMEM(patch_stream.shape, bf),
         pltpu.VMEM((T, rows, padded), bf),
@@ -367,7 +366,8 @@
         pltpu.VMEM((bytes_here, padded), jnp.float32),
         pltpu.VMEM(byte_states.shape, bf),
         sem((S,)), sem((H,)), sem((S,)), sem((S,)), sem((S,)), sem((S,)),
-        sem((S,)), sem((S,)), sem((S,)), sem((S,)), sem((S,)), sem((T, S // T)),
+        sem((S,)), sem((S,)), sem((S,)), sem((S,)), sem((S,)), sem((S,)), sem((S,)),
+        sem((T, S // T)),
         sem((T,)), sem((T,)), sem((T,)), sem((T,)), sem((6,)),
     ]
     hbm = pl.BlockSpec(memory_space=pl.ANY)

time: 55.7 us -> 41.1 us (0.74)
  Pallas kernels: 51.3 us -> 37.2 us
    pallas_call x1, Pallas kernels: 51.3 us -> 37.2 us  [fused_form(): pl.pallas_call(functools.partial(fused_kernel, (S, T, H, rows, local)), o...]
where the time goes in v2:
time: 41.1 us; the launch traced here: 40.9 us
  Pallas kernels  37.2 us (91%)
  local copies, waits for them, and re-layouts  3.12 us (8%)
  between operations  0.64 us (2%)
    pallas_call x1, Pallas kernels, fused_form(): pl.pallas_call(functools.partial(fused_kernel, (S, T, H, rows, local)), o...  37.2 us
    unnamed x2, local copies, waits for them, and re-layouts  3.12 us

profile of v2, /device:TPU:0, one launch (start us, length us, event | category | flops | bytes accessed | tf_op | source)
XLA Modules:
  0.0 40.9 jit_solution(6612642290712906892)
XLA Ops:
  0.6 37.2 %shard_map.95 = (bf16[48,1024]{1,0:T(8,128)(2,1)}, bf16[192,320]{1,0:T(8,128)(2,1)}) custom-call(bf16[48,512]{1,0:T(8,128)(2,1)} %q_hbm.1, bf16[48,512]{1,0:T(8,128)(2,1)} %k_hbm.1, bf16[48,512]{1,0:T(8,128)(2,1)} %v_hbm.1, bf16[48,1024]{1,0:T(8,128)(2,1)} %ps_hbm.1, bf16[512,512]{1,0:T(8,128)(2,1)} %ow_hbm.1, bf16[1024,1280]{1,0:T(8,128)(2,1)} %dw_hbm.1, ...), custom_call_target="tpu_custom_call" | custom-call | tf_op jit(solution)/shard_map/pallas_call | solution.py:374
  37.8 1.5 %copy.12 = bf16[48,1024]{1,0:T(8,128)(2,1)} copy(bf16[48,1024]{1,0:T(8,128)(2,1)} %get-tuple-element.4) | data formatting | bytes 196608
  39.4 1.6 %copy.13 = bf16[192,320]{1,0:T(8,128)(2,1)} copy(bf16[192,320]{1,0:T(8,128)(2,1)} %get-tuple-element.5) | data formatting | bytes 245760

commit v3 on v2

--- a/solution.py
+++ b/solution.py
@@ -94,7 +94,7 @@
     np_hbm, nb_hbm,
     qbuf, kbuf, vbuf, sbuf, aown, abuf, cbuf, rel, rbuf, npbuf, dsend, dbuf, lsend, lbuf,
     ow, dw, ps, bs, pd, nb,
-    qs, qr, ks, kr, vs, vr, ss, sr, as_, ar, cs, relr, fs, cr, ds_, dr, ls, lr, loc,
+    qs, qr, ks, kr, vs, vr, ss, sr, as_, ar, cs, relr, fs, cr, ds_, dr, ls, lr, loc, hello,
 ):
     S, T, H, rows, local = sizes
     G = S // H
@@ -123,11 +123,25 @@
         pl.semaphore_signal(
             barrier, inc=1, device_id={"seq": lax.rem(me + i, S), "tp": z}, device_id_type=MESH
         )
-    for i in range(1, T):
-        pl.semaphore_signal(
-            barrier, inc=1, device_id={"seq": me, "tp": lax.rem(z + i, T)}, device_id_type=MESH
-        )
-    pl.semaphore_wait(barrier, S + T - 2)
+
+    def greet(sem):
+        @pl.when(z > 0)
+        def _():
+            pl.semaphore_signal(
+                sem, inc=1, device_id={"seq": me, "tp": z - 1}, device_id_type=MESH
+            )
+
+        @pl.when(z < T - 1)
+        def _():
+            pl.semaphore_signal(
+                sem, inc=1, device_id={"seq": me, "tp": z + 1}, device_id_type=MESH
+            )
+
+    beside = jnp.where(z > 0, 1, 0) + jnp.where(z < T - 1, 1, 0)
+    greet(barrier)
+    pl.semaphore_wait(barrier, S - 1 + beside)
+    if T > 2:
+        greet(hello.at[0])
 
     def lanes(block, width):
         return pl.ds(pl.multiple_of(block * width, 128), width)
@@ -209,22 +223,29 @@
     )
     aown[...] = (summed / total).astype(jnp.bfloat16).reshape(H, rows, DH)
 
-    for e in range(G):
-        for jj in range(H):
-            i = jj * G + e
-            tgt = lax.rem(me + i, S)
-            dst = abuf.at[g, :, :, lanes(head, DH)]
-            if i == 0:
-                pltpu.make_async_copy(aown, dst, ar.at[me]).start()
-            else:
-                send(aown, dst, as_.at[i], ar.at[me], tgt, z)
+    own = abuf.at[g, :, :, lanes(head, DH)]
+    pltpu.make_async_copy(aown, own, ar.at[me]).start()
+    for jj in range(1, H):
+        tgt = lax.rem(head + jj, H) * G + g
+        send(aown, own, as_.at[jj * G], ar.at[me], tgt, z)
+    for e in range(1, G):
+        send(aown, own, as_.at[e], ar.at[me], head * G + lax.rem(g + e, G), z)
+    for n in range(1, T - 2):
+        pl.semaphore_wait(hello.at[n - 1], beside)
+        greet(hello.at[n])
     loads[0].wait()
 
     for e in range(G):
         gg = lax.rem(g + e, G)
         for jj in range(H):
-            src = lax.rem(head + jj, H) * G + gg
+            h = lax.rem(head - jj + H, H)
+            src = h * G + gg
             arrived(aown, ar.at[src])
+            if e == 0 and jj > 0:
+                piece = abuf.at[g, :, :, lanes(h, DH)]
+                for f in range(1, G):
+                    partner = head * G + lax.rem(g + f, G)
+                    send(piece, piece, as_.at[jj * G + f], ar.at[src], partner, z)
         product = jnp.dot(
             abuf[gg].reshape(mine, H * DH), ow[...], preferred_element_type=jnp.float32
         )
@@ -237,6 +258,8 @@
             else:
                 send(cbuf.at[gg, j], rel.at[me], cs.at[e * H + jj], relr.at[me], tgt, z)
 
+    if T > 2:
+        pl.semaphore_wait(hello.at[T - 3], beside)
     passed = []
     for e in range(G):
         for jj in range(H):
@@ -275,12 +298,11 @@
     padded = dbuf.shape[2]
     down = jnp.dot(npbuf[...], dw[...], preferred_element_type=jnp.float32)
 
-    def share(x, t):
-        turned = x if t == 0 else pltpu.roll(x, wide - t * local, 1)
-        return turned[:, :padded].astype(jnp.bfloat16)
+    def turned(x, t):
+        return (x if t == 0 else pltpu.roll(x, wide - t * local, 1))[:, :padded]
 
     for t in range(T):
-        dsend[t] = share(down, t)
+        dsend[t] = turned(down, t).astype(jnp.bfloat16)
     for i in range(1, T):
         t = lax.rem(z + i, T)
         send(dsend.at[t], dbuf.at[z], ds_.at[i], dr.at[z], me, t)
@@ -291,7 +313,7 @@
     pick = jnp.where(lane16 == held - 1.0, 1.0, 0.0).astype(jnp.bfloat16)
     last = jnp.dot(pick, down.astype(jnp.bfloat16), preferred_element_type=jnp.float32)
     for t in range(T):
-        lsend[t] = share(last, t)
+        lsend[t] = turned(last, t)[:1, :]
     after = lax.rem(me + 1, S)
     for i in range(T):
         t = lax.rem(z + i, T)
@@ -311,12 +333,12 @@
     for t in range(T):
         arrived(lbuf.at[t], lr.at[t])
     state = dbuf[0].astype(jnp.float32)
-    earlier = lbuf[0].astype(jnp.float32)
+    earlier = lbuf[0]
     for t in range(1, T):
         state = state + dbuf[t].astype(jnp.float32)
-        earlier = earlier + lbuf[t].astype(jnp.float32)
+        earlier = earlier + lbuf[t]
     state = state.astype(jnp.bfloat16)
-    earlier = earlier.astype(jnp.bfloat16).astype(jnp.float32)[:1, :]
+    earlier = earlier.astype(jnp.bfloat16).astype(jnp.float32)
     added = jnp.dot(member, state, preferred_element_type=jnp.float32)
     pd[...] = jnp.where(before, earlier, added)
     nb[...] = (bs[...].astype(jnp.float32) + pd[:, :local]).astype(jnp.bfloat16)
@@ -357,8 +379,8 @@
         pltpu.VMEM(patch_stream.shape, bf),
         pltpu.VMEM((T, rows, padded), bf),
         pltpu.VMEM((T, rows, padded), bf),
-        pltpu.VMEM((T, 16, padded), bf),
-        pltpu.VMEM((T, 16, padded), bf),
+        pltpu.VMEM((T, 1, padded), jnp.float32),
+        pltpu.VMEM((T, 1, padded), jnp.float32),
         pltpu.VMEM(out_weight.shape, bf),
         pltpu.VMEM(down_weight.shape, bf),
         pltpu.VMEM(patch_stream.shape, bf),
@@ -369,6 +391,7 @@
         sem((S,)), sem((S,)), sem((S,)), sem((S,)), sem((S,)), sem((S,)), sem((S,)),
         sem((T, S // T)),
         sem((T,)), sem((T,)), sem((T,)), sem((T,)), sem((6,)),
+        pltpu.SemaphoreType.REGULAR((max(T - 2, 1),)),
     ]
     hbm = pl.BlockSpec(memory_space=pl.ANY)
     return tuple(pl.pallas_call(

time: 41.1 us -> 39.7 us (0.966)
  Pallas kernels: 37.2 us -> 35.8 us
    pallas_call x1, Pallas kernels: 37.2 us -> 35.8 us  [fused_form(): pl.pallas_call(functools.partial(fused_kernel, (S, T, H, rows, local)), o...]
where the time goes in v3:
time: 39.7 us; the launch traced here: 39.6 us
  Pallas kernels  35.8 us (90%)
  local copies, waits for them, and re-layouts  3.12 us (8%)
  between operations  0.64 us (2%)
    pallas_call x1, Pallas kernels, fused_form(): pl.pallas_call(functools.partial(fused_kernel, (S, T, H, rows, local)), o...  35.8 us
    unnamed x2, local copies, waits for them, and re-layouts  3.12 us

profile of v3, /device:TPU:0, one launch (start us, length us, event | category | flops | bytes accessed | tf_op | source)
XLA Modules:
  0.0 39.6 jit_solution(2915909212061505094)
XLA Ops:
  0.6 35.8 %shard_map.95 = (bf16[48,1024]{1,0:T(8,128)(2,1)}, bf16[192,320]{1,0:T(8,128)(2,1)}) custom-call(bf16[48,512]{1,0:T(8,128)(2,1)} %q_hbm.1, bf16[48,512]{1,0:T(8,128)(2,1)} %k_hbm.1, bf16[48,512]{1,0:T(8,128)(2,1)} %v_hbm.1, bf16[48,1024]{1,0:T(8,128)(2,1)} %ps_hbm.1, bf16[512,512]{1,0:T(8,128)(2,1)} %ow_hbm.1, bf16[1024,1280]{1,0:T(8,128)(2,1)} %dw_hbm.1, ...), custom_call_target="tpu_custom_call" | custom-call | tf_op jit(solution)/shard_map/pallas_call | solution.py:397
  36.4 1.5 %copy.12 = bf16[48,1024]{1,0:T(8,128)(2,1)} copy(bf16[48,1024]{1,0:T(8,128)(2,1)} %get-tuple-element.4) | data formatting | bytes 196608
  38.0 1.6 %copy.13 = bf16[192,320]{1,0:T(8,128)(2,1)} copy(bf16[192,320]{1,0:T(8,128)(2,1)} %get-tuple-element.5) | data formatting | bytes 245760

commit v4 on v3

--- a/solution.py
+++ b/solution.py
@@ -90,10 +90,10 @@
 
 def fused_kernel(
     sizes,
-    q_hbm, k_hbm, v_hbm, ps_hbm, ow_hbm, dw_hbm, bs_hbm, st_ref,
-    np_hbm, nb_hbm,
-    qbuf, kbuf, vbuf, sbuf, aown, abuf, cbuf, rel, rbuf, npbuf, dsend, dbuf, lsend, lbuf,
-    ow, dw, ps, bs, pd, nb,
+    q_hbm, k_hbm, v_hbm, ps_hbm, ow_hbm, dw_hbm, bs_hbm, st_hbm,
+    np_out, nb_out,
+    qbuf, kbuf, vbuf, sbuf, aown, abuf, cbuf, rel, rbuf, dsend, dbuf, lsend, lbuf,
+    ow, dw, ps, bs, pd, st_ref,
     qs, qr, ks, kr, vs, vr, ss, sr, as_, ar, cs, relr, fs, cr, ds_, dr, ls, lr, loc, hello,
 ):
     S, T, H, rows, local = sizes
@@ -114,10 +114,8 @@
     for load in loads:
         load.start()
 
-    starts = jnp.broadcast_to(st_ref[...], (8, rows))
-    valid8 = jnp.where(starts < B_DEV, 1.0, 0.0)
-    sbuf[me] = valid8
-
+    first = pltpu.make_async_copy(st_hbm, st_ref, loc.at[4])
+    first.start()
     barrier = pltpu.get_barrier_semaphore()
     for i in range(1, S):
         pl.semaphore_signal(
@@ -139,6 +137,11 @@
 
     beside = jnp.where(z > 0, 1, 0) + jnp.where(z < T - 1, 1, 0)
     greet(barrier)
+    first.wait()
+    starts = jnp.broadcast_to(st_ref[...], (8, rows))
+    valid8 = jnp.where(starts < B_DEV, 1.0, 0.0)
+    sbuf[me] = valid8
+
     pl.semaphore_wait(barrier, S - 1 + beside)
     if T > 2:
         greet(hello.at[0])
@@ -289,14 +292,12 @@
         for t in range(1, T):
             mixed = mixed + rbuf[t, p].astype(jnp.float32)
         at = pl.ds(p * cols, cols)
-        npbuf[:, at] = (ps[:, at].astype(jnp.float32) + mixed).astype(jnp.bfloat16)
-    np_out = pltpu.make_async_copy(npbuf, np_hbm, loc.at[4])
-    np_out.start()
+        np_out[:, at] = (ps[:, at].astype(jnp.float32) + mixed).astype(jnp.bfloat16)
 
     loads[2].wait()
     wide = dw.shape[1]
     padded = dbuf.shape[2]
-    down = jnp.dot(npbuf[...], dw[...], preferred_element_type=jnp.float32)
+    down = jnp.dot(np_out[...], dw[...], preferred_element_type=jnp.float32)
 
     def turned(x, t):
         return (x if t == 0 else pltpu.roll(x, wide - t * local, 1))[:, :padded]
@@ -341,9 +342,7 @@
     earlier = earlier.astype(jnp.bfloat16).astype(jnp.float32)
     added = jnp.dot(member, state, preferred_element_type=jnp.float32)
     pd[...] = jnp.where(before, earlier, added)
-    nb[...] = (bs[...].astype(jnp.float32) + pd[:, :local]).astype(jnp.bfloat16)
-    nb_out = pltpu.make_async_copy(nb, nb_hbm, loc.at[5])
-    nb_out.start()
+    nb_out[...] = (bs[...].astype(jnp.float32) + pd[:, :local]).astype(jnp.bfloat16)
 
     for copy in sends:
         copy.wait_send()
@@ -351,8 +350,16 @@
     for away, onward in passed:
         pl.when(away)(onward.wait_send)
 
-    np_out.wait()
-    nb_out.wait()
+
+def put_out(np_ref, nb_ref, np_hbm, nb_hbm, sems):
+    copies = [
+        pltpu.make_async_copy(np_ref, np_hbm, sems.at[0]),
+        pltpu.make_async_copy(nb_ref, nb_hbm, sems.at[1]),
+    ]
+    for copy in copies:
+        copy.start()
+    for copy in copies:
+        copy.wait()
 
 
 def fused_form(
@@ -376,7 +383,6 @@
         pltpu.VMEM((G, H, rows, cols), bf),
         pltpu.VMEM((S, rows, cols), bf),
         pltpu.VMEM((T, S // T, rows, cols), bf),
-        pltpu.VMEM(patch_stream.shape, bf),
         pltpu.VMEM((T, rows, padded), bf),
         pltpu.VMEM((T, rows, padded), bf),
         pltpu.VMEM((T, 1, padded), jnp.float32),
@@ -386,25 +392,43 @@
         pltpu.VMEM(patch_stream.shape, bf),
         pltpu.VMEM(byte_states.shape, bf),
         pltpu.VMEM((bytes_here, padded), jnp.float32),
-        pltpu.VMEM(byte_states.shape, bf),
+        pltpu.VMEM(patch_starts.shape, jnp.int32),
         sem((S,)), sem((H,)), sem((S,)), sem((S,)), sem((S,)), sem((S,)),
         sem((S,)), sem((S,)), sem((S,)), sem((S,)), sem((S,)), sem((S,)), sem((S,)),
         sem((T, S // T)),
-        sem((T,)), sem((T,)), sem((T,)), sem((T,)), sem((6,)),
+        sem((T,)), sem((T,)), sem((T,)), sem((T,)), sem((5,)),
         pltpu.SemaphoreType.REGULAR((max(T - 2, 1),)),
     ]
-    hbm = pl.BlockSpec(memory_space=pl.ANY)
-    return tuple(pl.pallas_call(
+    hbm = pl.BlockSpec(memory_space=pltpu.HBM)
+    vmem = pl.BlockSpec(memory_space=pltpu.VMEM)
+    held = pl.pallas_call(
         functools.partial(fused_kernel, (S, T, H, rows, local)),
         out_shape=(
             jax.ShapeDtypeStruct(patch_stream.shape, bf),
             jax.ShapeDtypeStruct(byte_states.shape, bf),
         ),
-        in_specs=[hbm] * 7 + [pl.BlockSpec(memory_space=pltpu.VMEM)],
+        in_specs=[hbm] * 8,
+        out_specs=(vmem, vmem),
+        scratch_shapes=scratch,
+        compiler_params=pltpu.CompilerParams(collective_id=0, has_side_effects=True, vmem_limit_bytes=24 << 20),
+    )(*(
+        pltpu.with_memory_space_constraint(x, pltpu.HBM)
+        for x in (
+            queries, keys, values, patch_stream,
+            out_weight, down_weight, byte_states, patch_starts,
+        )
+    ))
+    return tuple(pl.pallas_call(
+        put_out,
+        out_shape=(
+            jax.ShapeDtypeStruct(patch_stream.shape, bf),
+            jax.ShapeDtypeStruct(byte_states.shape, bf),
+        ),
+        in_specs=[vmem, vmem],
         out_specs=(hbm, hbm),
-        scratch_shapes=scratch,
-        compiler_params=pltpu.CompilerParams(collective_id=0, has_side_effects=True),
-    )(queries, keys, values, patch_stream, out_weight, down_weight, byte_states, patch_starts))
+        scratch_shapes=[sem((2,))],
+        compiler_params=pltpu.CompilerParams(vmem_limit_bytes=4 << 20),
+    )(*held))
 
 
 def on_device(S, T, *args):

time: 39.7 us -> 36 us (0.907)
  local copies, waits for them, and re-layouts: 3.12 us -> 0 us
  Pallas kernels: 35.8 us -> 35.2 us
    unnamed x2 -> x0, local copies, waits for them, and re-layouts: 3.12 us -> none
    pallas_call x1, Pallas kernels: 35.8 us -> 34.5 us  [fused_form(): pl.pallas_call(functools.partial(fused_kernel, (S, T, H, rows, local)), o...]
    pallas_call x0 -> x1, Pallas kernels: none -> 0.71 us  [fused_form(): pl.pallas_call(put_out, out_shape=(jax.ShapeDtypeStruct(patch_stream.shap...]
where the time goes in v4:
time: 36 us; the launch traced here: 35.9 us
  Pallas kernels  35.2 us (98%)
  between operations  0.64 us (2%)
    pallas_call x1, Pallas kernels, fused_form(): pl.pallas_call(functools.partial(fused_kernel, (S, T, H, rows, local)), o...  34.5 us

profile of v4, /device:TPU:0, one launch (start us, length us, event | category | flops | bytes accessed | tf_op | source)
XLA Modules:
  0.0 35.9 jit_solution(2616703653894095192)
XLA Ops:
  0.6 34.5 %shard_map.95 = (bf16[48,1024]{1,0:T(8,128)(2,1)S(1)}, bf16[192,320]{1,0:T(8,128)(2,1)S(1)}) custom-call(bf16[48,512]{1,0:T(8,128)(2,1)} %q_hbm.1, bf16[48,512]{1,0:T(8,128)(2,1)} %k_hbm.1, bf16[48,512]{1,0:T(8,128)(2,1)} %v_hbm.1, bf16[48,1024]{1,0:T(8,128)(2,1)} %ps_hbm.1, bf16[512,512]{1,0:T(8,128)(2,1)} %ow_hbm.1, bf16[1024,1280]{1,0:T(8,128)(2,1)} %dw_hbm.1, ...), custom_call_target="tpu_custom_call" | custom-call | tf_op jit(solution)/shard_map/pallas_call | solution.py:404
  35.2 0.7 %shard_map.96 = (bf16[48,1024]{1,0:T(8,128)(2,1)}, bf16[192,320]{1,0:T(8,128)(2,1)}) custom-call(bf16[48,1024]{1,0:T(8,128)(2,1)S(1)} %get-tuple-element.4.np_ref, bf16[192,320]{1,0:T(8,128)(2,1)S(1)} %get-tuple-element.5.nb_ref), custom_call_target="tpu_custom_call" | custom-call | tf_op jit(solution)/shard_map/pallas_call | solution.py:421

commit v5 on v4

--- a/solution.py
+++ b/solution.py
@@ -284,20 +284,21 @@
             passed.append((away, onward))
 
     loads[1].wait()
-    for t in range(T):
-        for p in range(CP):
+    loads[2].wait()
+    wide = dw.shape[1]
+    padded = dbuf.shape[2]
+    down = jnp.zeros((rows, wide), jnp.float32)
+    for n in range(CP):
+        p = lax.rem(g + n, CP)
+        for t in range(T):
             arrived(rbuf.at[t, p], cr.at[t, p])
-    for p in range(CP):
         mixed = rbuf[0, p].astype(jnp.float32)
         for t in range(1, T):
             mixed = mixed + rbuf[t, p].astype(jnp.float32)
-        at = pl.ds(p * cols, cols)
-        np_out[:, at] = (ps[:, at].astype(jnp.float32) + mixed).astype(jnp.bfloat16)
-
-    loads[2].wait()
-    wide = dw.shape[1]
-    padded = dbuf.shape[2]
-    down = jnp.dot(np_out[...], dw[...], preferred_element_type=jnp.float32)
+        at = lanes(p, cols)
+        patches = (ps[:, at].astype(jnp.float32) + mixed).astype(jnp.bfloat16)
+        np_out[:, at] = patches
+        down = down + jnp.dot(patches, dw[at, :], preferred_element_type=jnp.float32)
 
     def turned(x, t):
         return (x if t == 0 else pltpu.roll(x, wide - t * local, 1))[:, :padded]

time: 36 us -> 35.9 us (level)
  no operation moved by 1% of the time
where the time goes in v5:
time: 35.9 us; the launch traced here: 35.8 us
  Pallas kernels  35.1 us (98%)
  between operations  0.64 us (2%)
    pallas_call x1, Pallas kernels, fused_form(): pl.pallas_call(functools.partial(fused_kernel, (S, T, H, rows, local)), o...  34.4 us

profile of v5, /device:TPU:0, one launch (start us, length us, event | category | flops | bytes accessed | tf_op | source)
XLA Modules:
  0.0 35.8 jit_solution(8124848349676220584)
XLA Ops:
  0.6 34.4 %shard_map.95 = (bf16[48,1024]{1,0:T(8,128)(2,1)S(1)}, bf16[192,320]{1,0:T(8,128)(2,1)S(1)}) custom-call(bf16[48,512]{1,0:T(8,128)(2,1)} %q_hbm.1, bf16[48,512]{1,0:T(8,128)(2,1)} %k_hbm.1, bf16[48,512]{1,0:T(8,128)(2,1)} %v_hbm.1, bf16[48,1024]{1,0:T(8,128)(2,1)} %ps_hbm.1, bf16[512,512]{1,0:T(8,128)(2,1)} %ow_hbm.1, bf16[1024,1280]{1,0:T(8,128)(2,1)} %dw_hbm.1, ...), custom_call_target="tpu_custom_call" | custom-call | tf_op jit(solution)/shard_map/pallas_call | solution.py:405
  35.1 0.7 %shard_map.96 = (bf16[48,1024]{1,0:T(8,128)(2,1)}, bf16[192,320]{1,0:T(8,128)(2,1)}) custom-call(bf16[48,1024]{1,0:T(8,128)(2,1)S(1)} %get-tuple-element.4.np_ref, bf16[192,320]{1,0:T(8,128)(2,1)S(1)} %get-tuple-element.5.nb_ref), custom_call_target="tpu_custom_call" | custom-call | tf_op jit(solution)/shard_map/pallas_call | solution.py:422
